TPU v7x, 32 devices: a whole 2x2x4 slice. The times are simulated.
32 devices in a mesh: grp: 2 (over y), ctx: 4 (over z), kvh: 2 (over x), sub: 2 (over core).
Axes of the slice: x: 2, y: 2, z: 4, core: 2. Of those that a mesh axis runs over, the one named last changes fastest.
Arguments:
- queries: bfloat16 [1024, 8, 8, 128], P(('grp', 'ctx'), 'kvh', 'sub'), parts along dimension 0
- new_keys: bfloat16 [1024, 8, 128], P(('grp', 'ctx'), 'kvh'), parts along dimension 0
- new_values: bfloat16 [1024, 8, 128], P(('grp', 'ctx'), 'kvh'), parts along dimension 0, may hold values from -6 to 6
- cache_keys: bfloat16 [16384, 8, 128], P(('grp', 'ctx'), 'kvh'), parts along dimension 0, may hold values from -16 to 16
- cache_values: bfloat16 [16384, 8, 128], P(('grp', 'ctx'), 'kvh'), parts along dimension 0, may hold values from -6 to 6
- vertical_pool: int32 [16], P(('grp', 'ctx')), parts along dimension 0, may hold values from 0 to 15, as said below
- vertical_lists: int32 [8, 6], P(('grp', 'ctx')), parts along dimension 0, may hold values from 0 to 7, as said below
- slash_lists: int32 [8, 2], P(('grp', 'ctx')), parts along dimension 0, may hold values from 0 to 1, as said below
- list_counts: int32 [8, 2], P(('grp', 'ctx')), parts along dimension 0, may hold values from 1 to 6, as said below
Outputs:
- attention: bfloat16 [1024, 8, 8, 128], P(('grp', 'ctx'), 'kvh', 'sub'), parts along dimension 0
There are 2 independent parts, one for each index of `grp`. A program takes and returns all parts, laid end to end along the dimension named above; each array names one. Nothing has to cross between parts.
Inputs may be any that keep to these rules, and one draw needn't show every extreme that they name: `vertical_pool`: the 2 entries of one index of ctx are distinct. `vertical_lists`: in row b the first list_counts[b, 0] entries are distinct; later entries are never read. `slash_lists`: row b begins with 0; its first list_counts[b, 1] entries are distinct and none exceeds b or 1 plus b modulo 1; later entries are never read. `list_counts`: column 0 lies between 1 and 6, column 1 between 1 and 2, each reached in every draw.
All inputs are finite; a program needn't handle non-finite values.
Results may differ from a plain program's by a relative error of at most 0.014.
Values may be sent and summed in bfloat16 or wider, within the bound.
No kernel may reach another device: no remote copies, remote signals or barrier semaphores. Data moves between devices by JAX's collectives and lax.ppermute only.
A program may use at most 64 MiB of HBM per device.

v0:
```python
import jax
import jax.numpy as jnp
from jax import lax
from jax.sharding import PartitionSpec as P

BLK = 128


group_width = 8


def from_behind(block, axis, distance):
    devices = range(lax.axis_size(axis))
    route = [(i - distance, i) for i in devices if i - distance in devices]
    return lax.ppermute(block, axis, route)


def block_update(carry_state, query_block, block_keys, block_values, visible):
    row_peak, row_total, numerator = carry_state
    score_scale = query_block.shape[-1] ** (-0.5)
    scores = (
        jnp.einsum("rkgd,ckd->rkgc", query_block, block_keys, preferred_element_type=jnp.float32)
        * score_scale
    )
    scores = jnp.where(visible, scores, -jnp.inf)
    new_peak = jnp.maximum(row_peak, jnp.max(scores, axis=3))
    factor = jnp.exp(row_peak - new_peak)
    weights = jnp.exp(scores - new_peak[..., None])
    row_total = row_total * factor + jnp.sum(weights, axis=3)
    numerator = numerator * factor[..., None] + jnp.einsum(
        "rkgc,ckd->rkgd",
        weights.astype(jnp.bfloat16),
        block_values,
        preferred_element_type=jnp.float32,
    )
    return (new_peak, row_total, numerator)


def blank_state(query_block):
    rows_shape = query_block.shape[:3]
    return (
        jnp.full(rows_shape, -jnp.inf, jnp.float32),
        jnp.zeros(rows_shape, jnp.float32),
        jnp.zeros(query_block.shape, jnp.float32),
    )


def vertical_range(
    carry_state, query_block, pool_keys, pool_values, entries, start_entry, stop_entry
):
    list_length = entries.shape[0]
    padded_length = -(-list_length // group_width) * group_width
    padded_entries = jnp.pad(entries, (0, padded_length - list_length))
    block_size = pool_keys.shape[1]
    kv_width = pool_keys.shape[2]
    head_dim = pool_keys.shape[3]
    first_group = start_entry // group_width
    last_group = jnp.where(
        stop_entry > start_entry, (stop_entry + group_width - 1) // group_width, first_group
    )

    def group_step(group_index, inner_state):
        base = group_index * group_width
        slots = lax.dynamic_slice_in_dim(padded_entries, base, group_width)
        places = base + jnp.arange(group_width, dtype=jnp.int32)
        live = (places >= start_entry) & (places < stop_entry)
        slots = jnp.where(live, slots, 0)
        group_keys = jnp.take(pool_keys, slots, axis=0).reshape(
            group_width * block_size, kv_width, head_dim
        )
        group_values = jnp.take(pool_values, slots, axis=0).reshape(
            group_width * block_size, kv_width, head_dim
        )
        visible = jnp.repeat(live, block_size)[None, None, None, :]
        return block_update(inner_state, query_block, group_keys, group_values, visible)

    return lax.fori_loop(first_group, last_group, group_step, carry_state)


def slash_range(
    carry_state, query_block, window_keys, window_values, entries, entry_count, window_base
):
    block_size = query_block.shape[0]
    row_ids = lax.broadcasted_iota(jnp.int32, (block_size, 1, 1, block_size), 0)
    col_ids = lax.broadcasted_iota(jnp.int32, (block_size, 1, 1, block_size), 3)
    causal = col_ids <= row_ids

    def slash_step(step_index, inner_state):
        offset = entries[step_index]
        target = window_base - offset
        return block_update(
            inner_state,
            query_block,
            window_keys[target],
            window_values[target],
            causal | (offset > 0),
        )

    return lax.fori_loop(0, entry_count, slash_step, carry_state)


def shards(
    queries,
    new_keys,
    new_values,
    cache_keys,
    cache_values,
    vertical_pool,
    vertical_lists,
    slash_lists,
    list_counts,
):
    queries = lax.all_to_all(queries, "sub", split_axis=1, concat_axis=2, tiled=True)
    kv_width = queries.shape[1]
    first_head = lax.axis_index("sub") * kv_width
    new_keys = lax.dynamic_slice_in_dim(new_keys, first_head, kv_width, 1)
    new_values = lax.dynamic_slice_in_dim(new_values, first_head, kv_width, 1)
    cache_keys = lax.dynamic_slice_in_dim(cache_keys, first_head, kv_width, 1)
    cache_values = lax.dynamic_slice_in_dim(cache_values, first_head, kv_width, 1)
    tokens, kv_width, groups, head_dim = queries.shape
    block_size = BLK
    query_count = tokens // block_size
    cache_count = cache_keys.shape[0] // block_size
    chosen_keys = jnp.take(
        cache_keys.reshape(cache_count, block_size, kv_width, head_dim), vertical_pool, axis=0
    )
    chosen_values = jnp.take(
        cache_values.reshape(cache_count, block_size, kv_width, head_dim), vertical_pool, axis=0
    )
    pool_keys, pool_values = (
        lax.all_gather(chosen_keys, "ctx", axis=0, tiled=True),
        lax.all_gather(chosen_values, "ctx", axis=0, tiled=True),
    )
    earlier_keys, earlier_values = from_behind((new_keys, new_values), "ctx", 1)
    window_keys = jnp.concatenate([earlier_keys, new_keys], 0).reshape(
        2 * query_count, block_size, kv_width, head_dim
    )
    window_values = jnp.concatenate([earlier_values, new_values], 0).reshape(
        2 * query_count, block_size, kv_width, head_dim
    )
    query_grid = queries.reshape(query_count, block_size, kv_width, groups, head_dim)
    query_block = query_grid[0]
    carry_state = vertical_range(
        blank_state(query_block),
        query_block,
        pool_keys,
        pool_values,
        vertical_lists[0],
        0,
        list_counts[0, 0],
    )
    carry_state = slash_range(
        carry_state,
        query_block,
        window_keys,
        window_values,
        slash_lists[0],
        list_counts[0, 1],
        query_count,
    )
    results = [(carry_state[2] / carry_state[1][..., None]).astype(jnp.bfloat16)]
    attention = jnp.stack(results).reshape(tokens, kv_width, groups, head_dim)
    attention = lax.all_to_all(attention, "sub", split_axis=2, concat_axis=1, tiled=True)
    return attention


def solution(mesh):
    in_specs = (
        P(("grp", "ctx"), "kvh", "sub", None),
        P(("grp", "ctx"), "kvh", None),
        P(("grp", "ctx"), "kvh", None),
        P(("grp", "ctx"), "kvh", None),
        P(("grp", "ctx"), "kvh", None),
        P(("grp", "ctx")),
        P(("grp", "ctx"), None),
        P(("grp", "ctx"), None),
        P(("grp", "ctx"), None),
    )
    out_specs = P(("grp", "ctx"), "kvh", "sub", None)
    return jax.shard_map(shards, mesh=mesh, in_specs=in_specs, out_specs=out_specs, check_vma=False)
```

profile of v0, /device:TPU:31, one launch (start us, length us, event | category | flops | bytes accessed | tf_op | source)
XLA Modules:
  0.0 80.9 jit_solution(13073453692627988629)
XLA Ops:
  0.0 2.0 %copy.62 = bf16[128,4,4,128]{3,2,0,1:T(4,128)(2,1)} copy(bf16[128,4,4,128]{3,2,1,0:T(4,128)(2,1)} %param.17) | data formatting | bytes 1048576 | tf_op args[0]
  2.1 4.2 %all-to-all-start = ((bf16[128,4,4,128]{3,2,0,1:T(4,128)(2,1)}), bf16[128,4,4,128]{3,2,0,1:T(4,128)(2,1)S(1)}, u32[]{:S(2)}, u32[]{:S(2)}) async-start(bf16[128,4,4,128]{3,2,0,1:T(4,128)(2,1)} %copy.62), calls=%async_computation | async-start | bytes 1048576 | tf_op jit(solution)/shard_map/all_to_all | solution.py:113
  6.2 0.1 constant_dynamic-slice_fusion.1
  6.3 1.3 %collective-permute-start = (bf16[128,2,128]{2,0,1:T(8,128)(2,1)S(1)}, bf16[128,2,128]{2,0,1:T(8,128)(2,1)S(1)}, u32[]{:S(2)}, u32[]{:S(2)}) collective-permute-start(bf16[128,2,128]{2,0,1:T(8,128)(2,1)S(1)} %copy.87), channel_id=1, source_target_pairs={{0,4},{4,8},{8,12},{1,5},{5,9},{9,13},{2,6},{6,10},{10,14},{3,7},{... | collective-permute-start | bytes 196616 | tf_op jit(solution)/shard_map/ppermute | solution.py:15
  7.6 1.0 %constant_dynamic-slice_fusion = bf16[128,2,128]{2,1,0:T(2,128)(2,1)S(1)} fusion(bf16[128,4,128]{2,1,0:T(4,128)(2,1)} %param.19, s32[]{:T(128)S(6)} %select_n.63), kind=kLoop, calls=%fused_computation.58 | loop fusion | bytes 131076 | tf_op jit(solution)/shard_map/dynamic_slice | solution.py:117
  8.6 1.3 %collective-permute-start.1 = (bf16[128,2,128]{2,0,1:T(8,128)(2,1)S(1)}, bf16[128,2,128]{2,0,1:T(8,128)(2,1)}, u32[]{:S(2)}, u32[]{:S(2)}) collective-permute-start(bf16[128,2,128]{2,0,1:T(8,128)(2,1)S(1)} %copy.88), channel_id=1, source_target_pairs={{0,4},{4,8},{8,12},{1,5},{5,9},{9,13},{2,6},{6,10},{10,14},{3,7},{... | collective-permute-start | bytes 196616 | tf_op jit(solution)/shard_map/ppermute | solution.py:15
  9.9 1.3 %fusion.36 = (s32[1,1]{1,0:T(1,128)}, s32[1,1]{1,0:T(1,128)}) fusion(s32[1,2]{1,0:T(1,128)} %param.25), kind=kLoop, calls=%fused_computation.63 | loop fusion | bytes 16 | tf_op jit(solution)/shard_map/slice | solution.py:158
  12.4 0.7 compare_select_fusion.1
  13.0 0.7 compare_and_fusion.2
  13.7 3.8 %constant_dynamic-slice_fusion.2 = (bf16[2048,2,128]{2,1,0:T(2,128)(2,1)S(1)}, bf16[2048,2,128]{2,1,0:T(2,128)(2,1)S(1)}) fusion(bf16[2048,4,128]{2,1,0:T(4,128)(2,1)} %param.21, s32[]{:T(128)S(6)} %select_n.63, bf16[2048,4,128]{2,1,0:T(4,128)(2,1)} %param.20), kind=kLoop, calls=%fused_computation.60 | loop fusion | bytes 4194308 | tf_op jit(solution)/shard_map/dynamic_slice | solution.py:119
  17.5 0.1 copy.89
  17.6 0.1 copy.61
  17.7 0.1 copy.90
  17.9 0.1 copy.65
  18.0 0.6 gather_fusion.2
  18.6 0.6 gather_fusion.3
  19.2 0.1 broadcast_select_fusion.2
  19.3 15.4 %all_gather.6 = bf16[8,128,2,128]{3,1,2,0:T(8,128)(2,1)S(1)} all-gather(bf16[2,128,2,128]{3,1,2,0:T(8,128)(2,1)S(1)} %get-tuple-element.337), channel_id=1, replica_groups=mesh['grp'=2,'ctx'=4,'kvh'=2,'sub'=2] {'ctx'}, dimensions={0}, use_global_device_ids=true | all-gather | bytes 655360 | tf_op jit(solution)/shard_map/all_gather | solution.py:131
  34.6 0.5 copy.66
  35.2 12.0 %all_gather.7 = bf16[8,128,2,128]{3,1,2,0:T(8,128)(2,1)S(1)} all-gather(bf16[2,128,2,128]{3,1,2,0:T(8,128)(2,1)S(1)} %get-tuple-element.336), channel_id=1, replica_groups=mesh['grp'=2,'ctx'=4,'kvh'=2,'sub'=2] {'ctx'}, dimensions={0}, use_global_device_ids=true | all-gather | bytes 655360 | tf_op jit(solution)/shard_map/all_gather | solution.py:132
  47.2 0.5 copy.67
  47.8 0.1 copy.63
  47.9 0.1 broadcast_in_dim.72
  48.1 0.0 copy-start.4
  48.1 10.8 %while.31 = (s32[]{:T(128)}, f32[128,2,8]{0,2,1:T(8,128)S(1)}, f32[128,2,8]{0,2,1:T(8,128)S(1)}, f32[128,2,8,128]{0,3,2,1:T(8,128)S(1)}, s32[]{:T(128)}, /*index...) while((s32[]{:T(128)}, f32[128,2,8]{0,2,1:T(8,128)S(1)}, ...), condition=%wide.region_3.6_spmd, body=%wide.region_0.5_spmd.sunk | while | flops 1097864192 | bytes 37364096 | solution.py:77
  48.3 0.0 copy-start.1
  48.3 0.6 compare_and_fusion.5
  48.9 1.6 %gather_fusion = bf16[8,128,2,128]{3,2,1,0:T(2,128)(2,1)S(1)} fusion(bf16[8,128,2,128]{3,2,1,0:T(2,128)(2,1)S(1)} %get-tuple-element.517, s32[1024]{0:T(1024)S(1)} %pad_clamp_fusion.3), kind=kCustom, calls=%fused_computation.3.clone.clone.1 | custom fusion | bytes 1048608 | tf_op jit(solution)/shard_map/while/body/jit(_take)/gather | solution.py:71
  50.5 1.6 %gather_fusion.1 = bf16[8,128,2,128]{3,2,1,0:T(2,128)(2,1)S(1)} fusion(bf16[8,128,2,128]{3,2,1,0:T(2,128)(2,1)S(1)} %get-tuple-element.515, s32[1024]{0:T(1024)S(1)} %pad_clamp_fusion.3), kind=kCustom, calls=%fused_computation.1.clone.clone.1 | custom fusion | bytes 1048608 | tf_op jit(solution)/shard_map/while/body/jit(_take)/gather | solution.py:68
  52.1 1.0 %broadcast_select_fusion.5 = (bf16[8,128,2,128]{3,2,1,0:T(2,128)(2,1)S(1)}, bf16[8,128,2,128]{3,2,1,0:T(2,128)(2,1)S(1)}) fusion(bf16[8,128,2,128]{3,2,1,0:T(2,128)(2,1)S(1)} %gather_fusion, pred[8]{0:T(512)(128)(4,1)S(1)} %get-tuple-element.464, bf16[8,128,2,128]{3,2,1,0:T(2,128)(2,1)S(1)} %gather_fusion.1), kind=kLoop, calls=%fused_computation.35.clone.1 | loop fusion | flops 524288 | bytes 2097160 | tf_op jit(solution)/shard_map/while/body/jit(_take)/select_n | solution.py:71
  53.1 0.1 broadcast_bitcast_fusion.2
  53.2 1.3 %bitcast_reduce_fusion.2 = (f32[128,2,8]{0,2,1:T(8,128)S(1)}, f32[2,1024,128,8]{2,1,3,0:T(8,128)S(1)}) fusion(pred[1024]{0:T(1024)(128)(4,1)S(1)} %broadcast_bitcast_fusion.2, bf16[128,2,8,128]{3,0,2,1:T(8,128)(2,1)S(1)} %get-tuple-element.516, bf16[1024,2,128,1]{2,1,0,3:T(2,128)(2,1)S(1)} %bitcast.107), kind=kOutput, calls=%fused_computation.26.clone.1 | convolution fusion | flops 543160320 | bytes 9446400 | tf_op jit(solution)/shard_map/while/body/rkgd,ckd->rkgc/dot_general | solution.py:22
  54.5 2.2 %fusion.54 = f32[128,2,8]{0,2,1:T(8,128)S(1)} fusion(f32[2,1024,128,8]{2,1,3,0:T(8,128)S(1)} %get-tuple-element.467, f32[128,2,8]{0,2,1:T(8,128)S(1)} %max.12, pred[1024]{0:T(1024)(128)(4,1)S(1)} %broadcast_bitcast_fusion.2), kind=kLoop, calls=%fused_computation.30.clone.1 | loop fusion | flops 8386560 | bytes 8406016 | tf_op jit(solution)/shard_map/while/body/reduce_sum | solution.py:29
  56.7 0.0 copy-start.2
  56.7 2.2 %fusion.55 = f32[128,2,8,128]{0,3,2,1:T(8,128)S(1)} fusion(f32[2,1024,128,8]{2,1,3,0:T(8,128)S(1)} %get-tuple-element.467, f32[128,2,8]{0,2,1:T(8,128)S(1)} %max.12, pred[1024]{0:T(1024)(128)(4,1)S(1)} %broadcast_bitcast_fusion.2, f32[128,2,8,128]{0,3,2,1:T(8,128)S(1)} %get-tuple-element.499, bf16[1024,2,128,1]{2,1,0,3:T(2,128)(2,1)S(1)} %bitcast.108, ...), kind=kOutput, calls=%fused_computation.34.clone.1 | convolution fusion | flops 545783808 | bytes 11027456 | tf_op jit(solution)/shard_map/while/body/rkgc,ckd->rkgd/dot_general | solution.py:30
  58.9 0.9 %pad_maximum_fusion.1 = bf16[256,2,128]{2,0,1:T(8,128)(2,1)S(1)} fusion(bf16[128,2,128]{2,0,1:T(8,128)(2,1)S(1)} %copy.88, bf16[128,2,128]{2,0,1:T(8,128)(2,1)} %collective-permute-done.1), kind=kLoop, calls=%fused_computation.52 | loop fusion | flops 262144 | bytes 262144 | tf_op jit(solution)/shard_map/concatenate | solution.py:138
  59.8 9.6 %while.32 = (s32[]{:T(128)}, f32[128,2,8]{0,2,1:T(8,128)S(1)}, f32[128,2,8]{0,2,1:T(8,128)S(1)}, f32[128,2,8,128]{0,3,2,1:T(8,128)S(1)}, s32[]{:T(128)}, /*index...) while((s32[]{:T(128)}, f32[128,2,8]{0,2,1:T(8,128)S(1)}, ...), condition=%wide.region_7.10_spmd.clone, body=%wide.region_4.9_spmd.clone.sunk | while | flops 136613888 | bytes 6062331 | solution.py:99
  60.5 0.7 dynamic_slice.57
  63.2 0.3 fusion.60
  63.5 0.2 fusion.61
  63.7 0.6 fusion.62
  65.0 0.7 dynamic_slice.57
  67.7 0.3 fusion.60
  68.0 0.2 fusion.61
  68.2 0.6 fusion.62
  69.4 0.1 fusion.34
  69.6 10.2 %all_to_all.36 = bf16[128,2,8,128]{0,3,1,2:T(8,128)(2,1)S(1)} all-to-all(bf16[128,2,8,128]{0,3,1,2:T(8,128)(2,1)S(1)} %fusion.34), channel_id=1, replica_groups=mesh['grp'=2,'ctx'=4,'kvh'=2,'sub'=2] {'sub'}, dimensions={2} | all-to-all | bytes 1048576 | tf_op jit(solution)/shard_map/all_to_all | solution.py:163
  79.7 1.2 %copy.74 = bf16[128,2,2,4,128]{4,3,2,1,0:T(4,128)(2,1)} copy(bf16[128,2,2,4,128]{0,4,2,3,1:T(8,128)(2,1)S(1)} %bitcast.112) | data formatting | bytes 1048576 | tf_op jit(solution)/shard_map/all_to_all | solution.py:163
  (30 shorter events, 0.2 us)
Async XLA Ops:
  0.0 6.2 %copy-start = (bf16[128,4,128]{2,1,0:T(4,128)(2,1)S(1)}, bf16[128,4,128]{2,1,0:T(4,128)(2,1)}, u32[]{:S(2)}) copy-start(bf16[128,4,128]{2,1,0:T(4,128)(2,1)} %param.18) | copy-start | bytes 393220
  2.1 45.7 %all-to-all-start = ((bf16[128,4,4,128]{3,2,0,1:T(4,128)(2,1)}), bf16[128,4,4,128]{3,2,0,1:T(4,128)(2,1)S(1)}, u32[]{:S(2)}, u32[]{:S(2)}) async-start(bf16[128,4,4,128]{3,2,0,1:T(4,128)(2,1)} %copy.62), calls=%async_computation | async-start | bytes 1048576 | tf_op jit(solution)/shard_map/all_to_all | solution.py:113
  6.3 52.6 %collective-permute-start = (bf16[128,2,128]{2,0,1:T(8,128)(2,1)S(1)}, bf16[128,2,128]{2,0,1:T(8,128)(2,1)S(1)}, u32[]{:S(2)}, u32[]{:S(2)}) collective-permute-start(bf16[128,2,128]{2,0,1:T(8,128)(2,1)S(1)} %copy.87), channel_id=1, source_target_pairs={{0,4},{4,8},{8,12},{1,5},{5,9},{9,13},{2,6},{6,10},{10,14},{3,7},{... | collective-permute-start | bytes 196616 | tf_op jit(solution)/shard_map/ppermute | solution.py:15
  8.6 50.3 %collective-permute-start.1 = (bf16[128,2,128]{2,0,1:T(8,128)(2,1)S(1)}, bf16[128,2,128]{2,0,1:T(8,128)(2,1)}, u32[]{:S(2)}, u32[]{:S(2)}) collective-permute-start(bf16[128,2,128]{2,0,1:T(8,128)(2,1)S(1)} %copy.88), channel_id=1, source_target_pairs={{0,4},{4,8},{8,12},{1,5},{5,9},{9,13},{2,6},{6,10},{10,14},{3,7},{... | collective-permute-start | bytes 196616 | tf_op jit(solution)/shard_map/ppermute | solution.py:15
  13.7 34.2 %copy-start.3 = (s32[1,6]{1,0:T(1,128)S(1)}, s32[1,6]{1,0:T(1,128)}, u32[]{:S(2)}) copy-start(s32[1,6]{1,0:T(1,128)} %param.23) | copy-start | bytes 76
  48.1 11.8 %copy-start.4 = (s32[1,2]{1,0:T(1,128)S(1)}, s32[1,2]{1,0:T(1,128)}, u32[]{:S(2)}) copy-start(s32[1,2]{1,0:T(1,128)} %param.24) | copy-start | bytes 28
  48.3 2.2 %copy-start.1 = (bf16[8,128,2,128]{3,2,1,0:T(2,128)(2,1)}, bf16[8,128,2,128]{3,2,1,0:T(2,128)(2,1)S(1)}, u32[]{:S(2)}) copy-start(bf16[8,128,2,128]{3,2,1,0:T(2,128)(2,1)S(1)} %get-tuple-element.517) | copy-start | bytes 1572868 | tf_op jit(solution)/shard_map/while
  56.7 2.2 %copy-start.2 = (bf16[8,128,2,128]{3,2,1,0:T(2,128)(2,1)S(1)}, bf16[8,128,2,128]{3,2,1,0:T(2,128)(2,1)}, u32[]{:S(2)}) copy-start(bf16[8,128,2,128]{3,2,1,0:T(2,128)(2,1)} %copy-done.1) | copy-start | bytes 1572868 | tf_op jit(solution)/shard_map/while
where the time goes:
time: 81.5 us; the launch traced here: 80.9 us
  blocking collectives  37.6 us (46%)
  local copies, waits for them, and re-layouts  17 us (21%)
  starting transfers between devices  6.74 us (8%)
  other arithmetic  6.58 us (8%)
  loops' own time  6.47 us (8%)
  matrix products  5.18 us (6%)
  between operations  1.4 us (2%)
    all_gather x1, blocking collectives, shards(): lax.all_gather(chosen_keys, 'ctx', axis=0, tiled=True)  15.4 us
    all_gather x1, blocking collectives, shards(): lax.all_gather(chosen_values, 'ctx', axis=0, tiled=True)  12 us
    all_to_all x1, blocking collectives, shards(): lax.all_to_all(attention, 'sub', split_axis=2, concat_axis=1, tiled=True)  10.2 us
    another operation x1, loops' own time, slash_range(): return lax.fori_loop(0, entry_count, slash_step, carry_state)  6.16 us
    all_to_all x1, starting transfers between devices, shards(): lax.all_to_all(queries, 'sub', split_axis=1, concat_axis=2, tiled=True)  4.15 us
    dynamic_slice x1, local copies, waits for them, and re-layouts, shards(): lax.dynamic_slice_in_dim(cache_values, first_head, kv_width, 1)  3.75 us
    dot_general x3, matrix products, block_update(): jnp.einsum('rkgc,ckd->rkgd', weights.astype(jnp.bfloat16), block_values,...  3.29 us
    ppermute x2, starting transfers between devices, from_behind(): return lax.ppermute(block, axis, route)  2.58 us
  transfers between devices with their start and end apart: 3, of which 0 were waited for; matrix products, arithmetic and copies ran while one was open for 26% of the time, Pallas kernels for 0%

commit v1 on v0

v1 whole, which is shorter than its diff:
```python
import functools
import math

import jax
import jax.numpy as jnp
from jax import lax
from jax.experimental import pallas as pl
from jax.experimental.pallas import tpu as pltpu
from jax.sharding import PartitionSpec as P

BLK = 128

VMEM = pltpu.VMEM
SMEM = pltpu.SMEM


def vmem_spec():
    return pl.BlockSpec(memory_space=VMEM)


def smem_spec():
    return pl.BlockSpec(memory_space=SMEM)


def hbm_spec():
    return pl.BlockSpec(memory_space=pl.ANY)


def split_heads(wide, rows, heads, block):
    return wide[pl.ds(block, rows, stride=heads), :].astype(jnp.bfloat16)


def gather_kernel(heads, per_core, pool, ck, cv, nk, nv, piece, fresh, raw, wide, sems, fresh_sem):
    core = lax.axis_index("sub")
    rows = BLK * heads
    copies = []
    for j in range(per_core):
        block = pool[core * per_core + j]
        for which, cache in enumerate((ck, cv)):
            copy = pltpu.make_async_copy(
                cache.at[block], raw.at[which * per_core + j], sems.at[which * per_core + j]
            )
            copy.start()
            copies.append(copy)

    @pl.when(core == 0)
    def _():
        pltpu.make_async_copy(nk, fresh, fresh_sem).start()

    @pl.when(core != 0)
    def _():
        pltpu.make_async_copy(nv, fresh, fresh_sem).start()

    for j in range(per_core):
        for which in range(2):
            copies[2 * j + which].wait()
            slot = which * per_core + j
            wide[slot] = raw[slot].astype(jnp.float32)
            for h in range(heads):
                piece[which, pl.ds((j * heads + h) * BLK, BLK), :] = split_heads(
                    wide.at[slot], BLK, heads, h
                )
    pltpu.make_async_copy(nk, fresh, fresh_sem).wait()


def gather(pool, ck, cv, nk, nv, heads, per_core):
    dim = ck.shape[-1]
    rows = BLK * heads
    slots = 2 * per_core
    return pl.pallas_call(
        functools.partial(gather_kernel, heads, per_core),
        out_shape=(
            jax.ShapeDtypeStruct((2, per_core * rows, dim), jnp.bfloat16),
            jax.ShapeDtypeStruct(nk.shape, jnp.bfloat16),
        ),
        in_specs=[smem_spec(), hbm_spec(), hbm_spec(), hbm_spec(), hbm_spec()],
        out_specs=(vmem_spec(), vmem_spec()),
        scratch_shapes=[
            VMEM((slots, rows, dim), jnp.bfloat16),
            VMEM((slots, rows, dim), jnp.float32),
            pltpu.SemaphoreType.DMA((slots,)),
            pltpu.SemaphoreType.DMA(()),
        ],
        name="gather",
    )(pool, ck, cv, nk, nv)


class Shape:
    def __init__(self, tokens, heads, groups, dim, vertical, cores):
        self.tokens, self.heads, self.groups, self.dim = tokens, heads, groups, dim
        self.rows = tokens * groups
        self.vertical, self.cores = vertical, cores
        self.per_core = vertical // cores
        self.scale = dim ** (-0.5) * math.log2(math.e)


def listed(entries, count, value):
    found = jnp.int32(0)
    for i in range(entries.shape[1]):
        hit = jnp.logical_and(i < count, entries[0, i] == value)
        found = jnp.maximum(found, hit.astype(jnp.int32))
    return found


def absorb(shape, q, m, acc, h, keys, values, lives, causal=False, first=False):
    dim = shape.dim
    scores = lax.dot_general(
        q[h], keys, (((1,), (1,)), ((), ())), preferred_element_type=jnp.float32
    )
    parts = []
    for i, live in enumerate(lives):
        part = scores[:, i * BLK : (i + 1) * BLK] * shape.scale
        if causal:
            row = lax.broadcasted_iota(jnp.int32, part.shape, 0) & (shape.tokens - 1)
            col = lax.broadcasted_iota(jnp.int32, part.shape, 1)
            part = jnp.where(col <= row, part, -jnp.inf)
        if live is not None:
            part = part + jnp.where(live > 0, 0.0, -jnp.inf)
        parts.append(part)
    highest = parts[0]
    for part in parts[1:]:
        highest = jnp.maximum(highest, part)
    highest = jnp.max(highest, axis=1, keepdims=True)
    if first:
        peak = jnp.broadcast_to(highest, (shape.rows, BLK))
    else:
        old = m[h]
        peak = jnp.maximum(old, highest)
    weights = jnp.concatenate(
        [jnp.exp2(part - peak).astype(jnp.bfloat16) for part in parts], axis=1
    )
    wide_values = jnp.concatenate([values, jnp.ones_like(values)], axis=1)
    added = jnp.dot(weights, wide_values, preferred_element_type=jnp.float32)
    if first:
        acc[h] = added
    else:
        factor = jnp.exp2(old - peak)
        acc[h] = acc[h] * jnp.concatenate([factor, factor], axis=1) + added
    m[h] = peak


def absorb_pieces(shape, vl, counts, q, m, acc, offset, pieces):
    owner = lax.axis_index("ctx") ^ offset
    core = lax.axis_index("sub")
    lives = []
    for away in range(shape.cores):
        source = core ^ away
        for j in range(shape.per_core):
            slot = owner * shape.vertical + source * shape.per_core + j
            lives.append(listed(vl, counts[0, 0], slot))
    any_live = functools.reduce(jnp.maximum, lives)

    @pl.when(any_live > 0)
    def _():
        for h in range(shape.heads):
            spans = [
                (piece, pl.ds((j * shape.heads + h) * BLK, BLK))
                for piece in pieces
                for j in range(shape.per_core)
            ]
            keys = jnp.concatenate([piece[0, span, :] for piece, span in spans], axis=0)
            values = jnp.concatenate([piece[1, span, :] for piece, span in spans], axis=0)
            absorb(shape, q, m, acc, h, keys, values, lives)


def finish(shape, acc, out, wide):
    stride = shape.heads * shape.groups
    for h in range(shape.heads):
        done = acc[h, :, : shape.dim] / acc[h, :, shape.dim :]
        for g in range(shape.groups):
            wide[pl.ds(h * shape.groups + g, shape.tokens, stride=stride), :] = done[
                g * shape.tokens : (g + 1) * shape.tokens
            ]
    out[...] = wide[...].astype(jnp.bfloat16)


def attend_kernel(shape, first, last, offsets, with_fresh, *refs):
    refs = list(refs)
    vl, sl, counts = refs[:3]
    refs = refs[3:]
    if first:
        raw_q, nk, nv = refs[:3]
        refs = refs[3:]
    else:
        q, m_in, acc_in = refs[:3]
        refs = refs[3:]
    if with_fresh:
        fresh = refs[: shape.cores]
        refs = refs[shape.cores :]
    pieces = []
    for _ in offsets:
        pieces.append(refs[: shape.cores])
        refs = refs[shape.cores :]
    if first:
        q, m, acc = refs[:3]
        refs = refs[3:]
    elif not last:
        m, acc = refs[:2]
        refs = refs[2:]
    else:
        out = refs[0]
        m, acc = refs[1:3]
        refs = refs[3:]
    wide_q, wide_kv = refs

    if first:
        stride = shape.heads * shape.groups
        wide_q[...] = raw_q[...].astype(jnp.float32)
        for h in range(shape.heads):
            for g in range(shape.groups):
                q[h, pl.ds(g * shape.tokens, shape.tokens), :] = split_heads(
                    wide_q, shape.tokens, stride, h * shape.groups + g
                )
        wide_kv[0] = nk[...].astype(jnp.float32)
        wide_kv[1] = nv[...].astype(jnp.float32)
        for h in range(shape.heads):
            keys = split_heads(wide_kv.at[0], BLK, shape.heads, h)
            values = split_heads(wide_kv.at[1], BLK, shape.heads, h)
            absorb(shape, q, m, acc, h, keys, values, [None], causal=True, first=True)
    else:
        m[...] = m_in[...]
        acc[...] = acc_in[...]

    if with_fresh:

        @pl.when(listed(sl, counts[0, 1], 1) > 0)
        def _():
            core = lax.axis_index("sub")
            for away in range(shape.cores):
                wide_kv[core ^ away] = fresh[away][...].astype(jnp.float32)
            for h in range(shape.heads):
                keys = split_heads(wide_kv.at[0], BLK, shape.heads, h)
                values = split_heads(wide_kv.at[1], BLK, shape.heads, h)
                absorb(shape, q, m, acc, h, keys, values, [None])

    for offset, arrays in zip(offsets, pieces):
        absorb_pieces(shape, vl, counts, q, m, acc, offset, arrays)

    if last:
        finish(shape, acc, out, wide_q)


def attend(shape, lists, state, offsets, pieces, fresh=(), first=False, last=False, name=None):
    stacked = (shape.heads, shape.rows)
    state_shapes = [
        jax.ShapeDtypeStruct(stacked + (BLK,), jnp.float32),
        jax.ShapeDtypeStruct(stacked + (2 * shape.dim,), jnp.float32),
    ]
    flat = shape.tokens * shape.heads * shape.groups
    scratch = [
        VMEM((flat, shape.dim), jnp.float32),
        VMEM((2, BLK * shape.heads, shape.dim), jnp.float32),
    ]
    aliases = {}
    if first:
        outs = [jax.ShapeDtypeStruct(stacked + (shape.dim,), jnp.bfloat16)] + state_shapes
    elif not last:
        outs = state_shapes
    else:
        outs = [jax.ShapeDtypeStruct((flat, shape.dim), jnp.bfloat16)]
        scratch = [VMEM(s.shape, s.dtype) for s in state_shapes] + scratch
    operands = [*lists, *state, *fresh, *[a for arrays in pieces for a in arrays]]
    return pl.pallas_call(
        functools.partial(attend_kernel, shape, first, last, offsets, bool(fresh)),
        out_shape=outs,
        in_specs=[smem_spec()] * 3 + [vmem_spec()] * (len(operands) - 3),
        out_specs=[vmem_spec()] * len(outs),
        scratch_shapes=scratch,
        input_output_aliases=aliases,
        compiler_params=pltpu.CompilerParams(vmem_limit_bytes=40 << 20),
        name=name,
    )(*operands)


def shards(mesh_shape, queries, nk, nv, ck, cv, pool, vl, sl, counts):
    n, cores = mesh_shape["ctx"], mesh_shape["sub"]
    tokens, heads, groups, dim = queries.shape
    shape = Shape(tokens, heads, groups, dim, pool.shape[0], cores)
    flat_q = queries.reshape(tokens * heads * groups, dim)
    flat_nk = nk.reshape(tokens * heads, dim)
    flat_nv = nv.reshape(tokens * heads, dim)
    blocks = ck.shape[0] // BLK
    flat_ck = ck.reshape(blocks, BLK * heads, dim)
    flat_cv = cv.reshape(blocks, BLK * heads, dim)
    lists = (vl, sl, counts)

    def exchange(x, away):
        return lax.ppermute(x, "ctx", [(i, i ^ away) for i in range(n)])

    def both(x):
        return [x] + [
            lax.ppermute(x, "sub", [(i, i ^ away) for i in range(cores)])
            for away in range(1, cores)
        ]

    own, fresh = gather(pool, flat_ck, flat_cv, flat_nk, flat_nv, heads, shape.per_core)
    held = {0: own}
    order = sorted(range(1, n), key=lambda o: (bin(o).count("1"), -o))
    for offset in order:
        low = offset & -offset
        held[offset] = exchange(held[offset ^ low], low)
    earlier = lax.ppermute(fresh, "ctx", [(i, i + 1) for i in range(n - 1)])

    state = attend(
        shape, lists, (flat_q, flat_nk, flat_nv), [0], [both(held[0])], first=True, name="local"
    )
    q = state[0]
    state = attend(
        shape, lists, state, order[:-1], [both(held[o]) for o in order[:-1]],
        fresh=both(earlier), name="middle",
    )
    (out,) = attend(
        shape, lists, (q, *state), order[-1:], [both(held[o]) for o in order[-1:]],
        last=True, name="tail",
    )
    return out.reshape(queries.shape)


def solution(mesh):
    mesh_shape = dict(mesh.shape)
    n, cores = mesh_shape["ctx"], mesh_shape["sub"]
    if n & (n - 1) or cores != 2:
        raise ValueError("unsupported mesh")
    split = ("grp", "ctx")
    in_specs = (
        P(split, "kvh", "sub", None),
        P(split, "kvh", None),
        P(split, "kvh", None),
        P(split, "kvh", None),
        P(split, "kvh", None),
        P(split),
        P(split, None),
        P(split, None),
        P(split, None),
    )
    out_specs = P(split, "kvh", "sub", None)
    return jax.shard_map(
        functools.partial(shards, mesh_shape),
        mesh=mesh,
        in_specs=in_specs,
        out_specs=out_specs,
        check_vma=False,
    )
```

time: 81.5 us -> 40.4 us (0.50)
  blocking collectives: 37.6 us -> 0 us
  waiting for transfers between devices: 0.01 us -> 20.1 us
  local copies, waits for them, and re-layouts: 17 us -> 0.97 us
  Pallas kernels: 0 us -> 12.6 us
  other arithmetic: 6.58 us -> 0 us
  loops' own time: 6.47 us -> 0 us
  matrix products: 5.18 us -> 0 us
  between operations: 1.4 us -> 0.14 us
    all_gather x2 -> x0, blocking collectives: 27.4 us -> none  [the longest x1 15.4 us: shards(): lax.all_gather(chosen_keys, 'ctx', axis=0, tiled=True)]
    ppermute x2 -> x9, waiting for transfers between devices: 0.01 us -> 20.1 us  [the longest x3 19.6 us: exchange(): return lax.ppermute(x, 'ctx', [(i, i ^ away) for i in range(n)])]
    pallas_call x0 -> x4, Pallas kernels: none -> 12.6 us  [the longest x3 9.97 us: attend(): pl.pallas_call(functools.partial(attend_kernel, shape, first, last, offse...]
    all_to_all x1 -> x0, blocking collectives: 10.2 us -> none  [shards(): lax.all_to_all(attention, 'sub', split_axis=2, concat_axis=1, tiled=True)]
    another operation x2 -> x0, loops' own time: 6.47 us -> none  [the longest x1 6.16 us: slash_range(): return lax.fori_loop(0, entry_count, slash_step, carry_state)]
    dynamic_slice x5 -> x0, local copies, waits for them, and re-layouts: 6.12 us -> none  [the longest x1 3.75 us: shards(): lax.dynamic_slice_in_dim(cache_values, first_head, kv_width, 1)]
    dot_general x6 -> x0, matrix products: 5.18 us -> none  [the longest x3 3.29 us: block_update(): jnp.einsum('rkgc,ckd->rkgd', weights.astype(jnp.bfloat16), block_values,...]
    gather x4 -> x0, local copies, waits for them, and re-layouts: 4.35 us -> none  [the longest x1 1.6 us: group_step(): jnp.take(pool_values, slots, axis=0)]
  transfers between devices with their start and end apart: 3 -> 9, of which waited for: 0 -> 3; matrix products, arithmetic and copies ran while one was open for 26% -> 0% of each run, Pallas kernels for 0% -> 17%
where the time goes in v1:
time: 40.4 us; the launch traced here: 40.2 us
  waiting for transfers between devices  20.1 us (50%)
  Pallas kernels  12.6 us (31%)
  starting transfers between devices  6.31 us (16%)
  local copies, waits for them, and re-layouts  0.97 us (2%)
    ppermute x3, waiting for transfers between devices, exchange(): return lax.ppermute(x, 'ctx', [(i, i ^ away) for i in range(n)])  19.6 us
    pallas_call x3, Pallas kernels, attend(): pl.pallas_call(functools.partial(attend_kernel, shape, first, last, offse...  9.97 us
    ppermute x5, starting transfers between devices, both(): lax.ppermute(x, 'sub', [(i, i ^ away) for i in range(cores)])  4.71 us
    pallas_call x1, Pallas kernels, gather(): pl.pallas_call(functools.partial(gather_kernel, heads, per_core), out_sha...  2.65 us
    ppermute x1, starting transfers between devices, shards(): earlier = lax.ppermute(fresh, 'ctx', [(i, i + 1) for i in range(n - 1)])  1.28 us
    unnamed x14, local copies, waits for them, and re-layouts  0.97 us
  transfers between devices with their start and end apart: 9, of which 3 were waited for; matrix products, arithmetic and copies ran while one was open for 0% of the time, Pallas kernels for 17%

profile of v1, /device:TPU:31, one launch (start us, length us, event | category | flops | bytes accessed | tf_op | source)
XLA Modules:
  0.0 40.2 jit_solution(4513151411042445959)
XLA Ops:
  0.0 0.0 copy-start
  0.0 0.0 copy-start.1
  0.0 0.0 copy-start.2
  0.0 0.0 copy-start.4
  0.0 0.0 copy-start.5
  0.0 0.0 copy-start.6
  0.0 2.6 %gather.1 = (bf16[2,512,128]{2,1,0:T(8,128)(2,1)}, bf16[512,128]{1,0:T(8,128)(2,1)}) custom-call(s32[2]{0:T(128)} %pool.1, bf16[16,512,128]{2,1,0:T(8,128)(2,1)} %bitcast.11, bf16[16,512,128]{2,1,0:T(8,128)(2,1)} %bitcast.12, bf16[512,128]{1,0:T(8,128)(2,1)} %bitcast.7, bf16[512,128]{1,0:T(8,128)(2,1)} %bitcast.9), custom_call_target="tpu_custom_call" | custom-call | tf_op jit(solution)/shard_map/gather/pallas_call | solution.py:70
  2.7 0.1 collective-permute-start.3
  2.8 0.2 collective-permute-start.5
  3.0 14.6 %collective-permute-done.3.refs_8_ = bf16[2,512,128]{2,1,0:T(8,128)(2,1)S(1)} collective-permute-done((bf16[2,512,128]{2,1,0:T(8,128)(2,1)}, bf16[2,512,128]{2,1,0:T(8,128)(2,1)S(1)}, u32[]{:S(2)}, u32[]{:S(2)}) %collective-permute-start.3) | collective-permute-done | bytes 262176 | tf_op jit(solution)/shard_map/ppermute | solution.py:288
  17.6 0.0 collective-permute-start.7
  17.6 0.5 %collective-permute-start = (bf16[2,512,128]{2,1,0:T(8,128)(2,1)}, bf16[2,512,128]{2,1,0:T(8,128)(2,1)S(1)}, u32[]{:S(2)}, u32[]{:S(2)}) collective-permute-start(bf16[2,512,128]{2,1,0:T(8,128)(2,1)} %get-tuple-element.12.refs_6_), channel_id=1, source_target_pairs={{0,1},{1,0},{2,3},{3,2},{4,5},{5,4},{6,7},{7,6},{8,9},{9,8},{10,11... | collective-permute-start | bytes 786440 | tf_op jit(solution)/shard_map/ppermute | solution.py:292
  18.1 1.3 %collective-permute-start.1 = (bf16[512,128]{1,0:T(8,128)(2,1)}, bf16[512,128]{1,0:T(8,128)(2,1)S(1)}, u32[]{:S(2)}, u32[]{:S(2)}) collective-permute-start(bf16[512,128]{1,0:T(8,128)(2,1)} %get-tuple-element.16), channel_id=1, source_target_pairs={{0,4},{4,8},{8,12},{1,5},{5,9},{9,13},{2,6},{6,10},{10,14},{3,7},{... | collective-permute-start | bytes 393224 | tf_op jit(solution)/shard_map/ppermute | solution.py:302
  19.4 0.1 collective-permute-start.4
  19.5 0.0 collective-permute-done.5.refs_10_
  19.5 0.5 %collective-permute-start.6 = (bf16[2,512,128]{2,1,0:T(8,128)(2,1)S(1)}, bf16[2,512,128]{2,1,0:T(8,128)(2,1)S(1)}, u32[]{:S(2)}, u32[]{:S(2)}) collective-permute-start(bf16[2,512,128]{2,1,0:T(8,128)(2,1)S(1)} %collective-permute-done.5.refs_10_), channel_id=1, source_target_pairs={{0,1},{1,0},{2,3},{3,2},{4,5},{5,4},{6,7},{7,6},{8,9},{9,8},{10,11... | collective-permute-start | bytes 786440 | tf_op jit(solution)/shard_map/ppermute | solution.py:292
  20.0 5.0 %collective-permute-done.7.refs_6_ = bf16[2,512,128]{2,1,0:T(8,128)(2,1)S(1)} collective-permute-done((bf16[2,512,128]{2,1,0:T(8,128)(2,1)S(1)}, bf16[2,512,128]{2,1,0:T(8,128)(2,1)S(1)}, u32[]{:S(2)}, u32[]{:S(2)}) %collective-permute-start.7) | collective-permute-done | bytes 262176 | tf_op jit(solution)/shard_map/ppermute | solution.py:288
  25.0 2.3 %collective-permute-start.8 = (bf16[2,512,128]{2,1,0:T(8,128)(2,1)S(1)}, bf16[2,512,128]{2,1,0:T(8,128)(2,1)S(1)}, u32[]{:S(2)}, u32[]{:S(2)}) collective-permute-start(bf16[2,512,128]{2,1,0:T(8,128)(2,1)S(1)} %collective-permute-done.7.refs_6_), channel_id=1, source_target_pairs={{0,1},{1,0},{2,3},{3,2},{4,5},{5,4},{6,7},{7,6},{8,9},{9,8},{10,11... | collective-permute-start | bytes 786440 | tf_op jit(solution)/shard_map/ppermute | solution.py:292
  27.3 0.5 %collective-permute-done.1.refs_6_ = bf16[512,128]{1,0:T(8,128)(2,1)S(1)} collective-permute-done((bf16[512,128]{1,0:T(8,128)(2,1)}, bf16[512,128]{1,0:T(8,128)(2,1)S(1)}, u32[]{:S(2)}, u32[]{:S(2)}) %collective-permute-start.1) | collective-permute-done | bytes 131104 | tf_op jit(solution)/shard_map/ppermute | solution.py:302
  27.8 1.3 %collective-permute-start.2 = (bf16[512,128]{1,0:T(8,128)(2,1)S(1)}, bf16[512,128]{1,0:T(8,128)(2,1)S(1)}, u32[]{:S(2)}, u32[]{:S(2)}) collective-permute-start(bf16[512,128]{1,0:T(8,128)(2,1)S(1)} %collective-permute-done.1.refs_6_), channel_id=1, source_target_pairs={{0,1},{1,0},{2,3},{3,2},{4,5},{5,4},{6,7},{7,6},{8,9},{9,8},{10,11... | collective-permute-start | bytes 393224 | tf_op jit(solution)/shard_map/ppermute | solution.py:292
  29.1 0.0 collective-permute-done.refs_7_
  29.1 0.0 copy-done
  29.1 0.0 copy-done.1
  29.1 0.0 copy-done.2
  29.2 0.0 copy-done.4
  29.2 0.0 copy-done.5
  29.2 0.0 copy-done.6
  29.2 0.0 copy-start.3
  29.2 0.9 %copy-done.3 = bf16[2,512,128]{2,1,0:T(8,128)(2,1)S(1)} copy-done((bf16[2,512,128]{2,1,0:T(8,128)(2,1)S(1)}, bf16[2,512,128]{2,1,0:T(8,128)(2,1)}, u32[]{:S(2)}) %copy-start.3) | copy-done | bytes 262168
  30.1 2.9 %local.1 = (bf16[4,512,128]{2,1,0:T(8,128)(2,1)S(1)}, f32[4,512,128]{2,1,0:T(8,128)S(1)}, f32[4,512,256]{2,1,0:T(8,128)S(1)}) custom-call(s32[1,6]{1,0:T(1,128)S(1)} %copy-done.4, s32[1,2]{1,0:T(1,128)S(1)} %copy-done.5, s32[1,2]{1,0:T(1,128)S(1)} %copy-done.6, bf16[2048,128]{1,0:T(8,128)(2,1)S(1)} %bitcast.6, bf16[512,128]{1,0:T(8,128)(2,1)S(1)} %bitcast.8, ...), custom_call_target="tpu_custom_call" | custom-call | tf_op jit(solution)/shard_map/local/pallas_call | solution.py:263
  33.0 0.0 collective-permute-done.2.refs_7_
  33.0 0.0 collective-permute-done.4.refs_9_
  33.0 0.0 collective-permute-done.6.refs_11_
  33.0 4.0 %middle.1 = (f32[4,512,128]{2,1,0:T(8,128)S(1)}, f32[4,512,256]{2,1,0:T(8,128)S(1)}) custom-call(s32[1,6]{1,0:T(1,128)S(1)} %copy-done.4, s32[1,2]{1,0:T(1,128)S(1)} %copy-done.5, s32[1,2]{1,0:T(1,128)S(1)} %copy-done.6, bf16[4,512,128]{2,1,0:T(8,128)(2,1)S(1)} %get-tuple-element.13.refs_3_, f32[4,512,128]{2,1,0:T(8,128)S(1)} %get-tuple-element.14.refs_4_, ...), custom_call_target="tpu_custom_call" | custom-call | tf_op jit(solution)/shard_map/middle/pallas_call | solution.py:263
  37.0 0.0 collective-permute-done.8.refs_7_
  37.0 3.1 %tail.1 = bf16[2048,128]{1,0:T(8,128)(2,1)} custom-call(s32[1,6]{1,0:T(1,128)S(1)} %copy-done.4, s32[1,2]{1,0:T(1,128)S(1)} %copy-done.5, s32[1,2]{1,0:T(1,128)S(1)} %copy-done.6, bf16[4,512,128]{2,1,0:T(8,128)(2,1)S(1)} %get-tuple-element.13.refs_3_, f32[4,512,128]{2,1,0:T(8,128)S(1)} %get-tuple-element.17.refs_4_, ...), custom_call_target="tpu_custom_call" | custom-call | tf_op jit(solution)/shard_map/tail/pallas_call | solution.py:263
Async XLA Ops:
  0.0 29.1 %copy-start = (bf16[128,4,4,128]{3,2,1,0:T(4,128)(2,1)S(1)}, bf16[128,4,4,128]{3,2,1,0:T(4,128)(2,1)}, u32[]{:S(2)}) copy-start(bf16[128,4,4,128]{3,2,1,0:T(4,128)(2,1)} %param.9) | copy-start | bytes 1572868
  0.0 29.1 %copy-start.1 = (bf16[128,4,128]{2,1,0:T(4,128)(2,1)S(1)}, bf16[128,4,128]{2,1,0:T(4,128)(2,1)}, u32[]{:S(2)}) copy-start(bf16[128,4,128]{2,1,0:T(4,128)(2,1)} %param.10) | copy-start | bytes 393220
  0.0 29.1 %copy-start.2 = (bf16[128,4,128]{2,1,0:T(4,128)(2,1)S(1)}, bf16[128,4,128]{2,1,0:T(4,128)(2,1)}, u32[]{:S(2)}) copy-start(bf16[128,4,128]{2,1,0:T(4,128)(2,1)} %param.11) | copy-start | bytes 393220
  0.0 29.1 %copy-start.4 = (s32[1,6]{1,0:T(1,128)S(1)}, s32[1,6]{1,0:T(1,128)}, u32[]{:S(2)}) copy-start(s32[1,6]{1,0:T(1,128)} %refs_0_.5) | copy-start | bytes 76
  0.0 29.1 %copy-start.5 = (s32[1,2]{1,0:T(1,128)S(1)}, s32[1,2]{1,0:T(1,128)}, u32[]{:S(2)}) copy-start(s32[1,2]{1,0:T(1,128)} %refs_1_.5) | copy-start | bytes 28
  0.0 29.1 %copy-start.6 = (s32[1,2]{1,0:T(1,128)S(1)}, s32[1,2]{1,0:T(1,128)}, u32[]{:S(2)}) copy-start(s32[1,2]{1,0:T(1,128)} %refs_2_.5) | copy-start | bytes 28
  2.7 14.9 %collective-permute-start.3 = (bf16[2,512,128]{2,1,0:T(8,128)(2,1)}, bf16[2,512,128]{2,1,0:T(8,128)(2,1)S(1)}, u32[]{:S(2)}, u32[]{:S(2)}) collective-permute-start(bf16[2,512,128]{2,1,0:T(8,128)(2,1)} %get-tuple-element.12.refs_6_), channel_id=1, source_target_pairs={{0,8},{4,12},{8,0},{12,4},{1,9},{5,13},{9,1},{13,5},{2,10},{6,14},... | collective-permute-start | bytes 786440 | tf_op jit(solution)/shard_map/ppermute | solution.py:288
  2.8 16.7 %collective-permute-start.5 = (bf16[2,512,128]{2,1,0:T(8,128)(2,1)}, bf16[2,512,128]{2,1,0:T(8,128)(2,1)S(1)}, u32[]{:S(2)}, u32[]{:S(2)}) collective-permute-start(bf16[2,512,128]{2,1,0:T(8,128)(2,1)} %get-tuple-element.12.refs_6_), channel_id=1, source_target_pairs={{0,4},{4,0},{8,12},{12,8},{1,5},{5,1},{9,13},{13,9},{2,6},{6,2},{1... | collective-permute-start | bytes 786440 | tf_op jit(solution)/shard_map/ppermute | solution.py:288
  17.6 7.4 %collective-permute-start.7 = (bf16[2,512,128]{2,1,0:T(8,128)(2,1)S(1)}, bf16[2,512,128]{2,1,0:T(8,128)(2,1)S(1)}, u32[]{:S(2)}, u32[]{:S(2)}) collective-permute-start(bf16[2,512,128]{2,1,0:T(8,128)(2,1)S(1)} %collective-permute-done.3.refs_8_), channel_id=1, source_target_pairs={{0,4},{4,0},{8,12},{12,8},{1,5},{5,1},{9,13},{13,9},{2,6},{6,2},{1... | collective-permute-start | bytes 786440 | tf_op jit(solution)/shard_map/ppermute | solution.py:288
  17.6 11.5 %collective-permute-start = (bf16[2,512,128]{2,1,0:T(8,128)(2,1)}, bf16[2,512,128]{2,1,0:T(8,128)(2,1)S(1)}, u32[]{:S(2)}, u32[]{:S(2)}) collective-permute-start(bf16[2,512,128]{2,1,0:T(8,128)(2,1)} %get-tuple-element.12.refs_6_), channel_id=1, source_target_pairs={{0,1},{1,0},{2,3},{3,2},{4,5},{5,4},{6,7},{7,6},{8,9},{9,8},{10,11... | collective-permute-start | bytes 786440 | tf_op jit(solution)/shard_map/ppermute | solution.py:292
  18.1 9.7 %collective-permute-start.1 = (bf16[512,128]{1,0:T(8,128)(2,1)}, bf16[512,128]{1,0:T(8,128)(2,1)S(1)}, u32[]{:S(2)}, u32[]{:S(2)}) collective-permute-start(bf16[512,128]{1,0:T(8,128)(2,1)} %get-tuple-element.16), channel_id=1, source_target_pairs={{0,4},{4,8},{8,12},{1,5},{5,9},{9,13},{2,6},{6,10},{10,14},{3,7},{... | collective-permute-start | bytes 393224 | tf_op jit(solution)/shard_map/ppermute | solution.py:302
  19.4 13.6 %collective-permute-start.4 = (bf16[2,512,128]{2,1,0:T(8,128)(2,1)S(1)}, bf16[2,512,128]{2,1,0:T(8,128)(2,1)S(1)}, u32[]{:S(2)}, u32[]{:S(2)}) collective-permute-start(bf16[2,512,128]{2,1,0:T(8,128)(2,1)S(1)} %collective-permute-done.3.refs_8_), channel_id=1, source_target_pairs={{0,1},{1,0},{2,3},{3,2},{4,5},{5,4},{6,7},{7,6},{8,9},{9,8},{10,11... | collective-permute-start | bytes 786440 | tf_op jit(solution)/shard_map/ppermute | solution.py:292
  19.5 13.6 %collective-permute-start.6 = (bf16[2,512,128]{2,1,0:T(8,128)(2,1)S(1)}, bf16[2,512,128]{2,1,0:T(8,128)(2,1)S(1)}, u32[]{:S(2)}, u32[]{:S(2)}) collective-permute-start(bf16[2,512,128]{2,1,0:T(8,128)(2,1)S(1)} %collective-permute-done.5.refs_10_), channel_id=1, source_target_pairs={{0,1},{1,0},{2,3},{3,2},{4,5},{5,4},{6,7},{7,6},{8,9},{9,8},{10,11... | collective-permute-start | bytes 786440 | tf_op jit(solution)/shard_map/ppermute | solution.py:292
  25.0 12.0 %collective-permute-start.8 = (bf16[2,512,128]{2,1,0:T(8,128)(2,1)S(1)}, bf16[2,512,128]{2,1,0:T(8,128)(2,1)S(1)}, u32[]{:S(2)}, u32[]{:S(2)}) collective-permute-start(bf16[2,512,128]{2,1,0:T(8,128)(2,1)S(1)} %collective-permute-done.7.refs_6_), channel_id=1, source_target_pairs={{0,1},{1,0},{2,3},{3,2},{4,5},{5,4},{6,7},{7,6},{8,9},{9,8},{10,11... | collective-permute-start | bytes 786440 | tf_op jit(solution)/shard_map/ppermute | solution.py:292
  27.8 5.2 %collective-permute-start.2 = (bf16[512,128]{1,0:T(8,128)(2,1)S(1)}, bf16[512,128]{1,0:T(8,128)(2,1)S(1)}, u32[]{:S(2)}, u32[]{:S(2)}) collective-permute-start(bf16[512,128]{1,0:T(8,128)(2,1)S(1)} %collective-permute-done.1.refs_6_), channel_id=1, source_target_pairs={{0,1},{1,0},{2,3},{3,2},{4,5},{5,4},{6,7},{7,6},{8,9},{9,8},{10,11... | collective-permute-start | bytes 393224 | tf_op jit(solution)/shard_map/ppermute | solution.py:292
  29.2 1.0 %copy-start.3 = (bf16[2,512,128]{2,1,0:T(8,128)(2,1)S(1)}, bf16[2,512,128]{2,1,0:T(8,128)(2,1)}, u32[]{:S(2)}) copy-start(bf16[2,512,128]{2,1,0:T(8,128)(2,1)} %get-tuple-element.12.refs_6_) | copy-start | bytes 786436

commit v2 on v1

--- a/solution.py
+++ b/solution.py
@@ -8,6 +8,7 @@
 from jax.experimental.pallas import tpu as pltpu
 from jax.sharding import PartitionSpec as P
 
+
 BLK = 128
 
 VMEM = pltpu.VMEM
@@ -32,7 +33,6 @@
 
 def gather_kernel(heads, per_core, pool, ck, cv, nk, nv, piece, fresh, raw, wide, sems, fresh_sem):
     core = lax.axis_index("sub")
-    rows = BLK * heads
     copies = []
     for j in range(per_core):
         block = pool[core * per_core + j]
@@ -102,8 +102,7 @@
     return found
 
 
-def absorb(shape, q, m, acc, h, keys, values, lives, causal=False, first=False):
-    dim = shape.dim
+def absorb(shape, q, m, acc, h, keys, values, lives, causal=False, first=False, keep=True):
     scores = lax.dot_general(
         q[h], keys, (((1,), (1,)), ((), ())), preferred_element_type=jnp.float32
     )
@@ -130,16 +129,17 @@
         [jnp.exp2(part - peak).astype(jnp.bfloat16) for part in parts], axis=1
     )
     wide_values = jnp.concatenate([values, jnp.ones_like(values)], axis=1)
-    added = jnp.dot(weights, wide_values, preferred_element_type=jnp.float32)
-    if first:
-        acc[h] = added
-    else:
+    total = jnp.dot(weights, wide_values, preferred_element_type=jnp.float32)
+    if not first:
         factor = jnp.exp2(old - peak)
-        acc[h] = acc[h] * jnp.concatenate([factor, factor], axis=1) + added
-    m[h] = peak
-
-
-def absorb_pieces(shape, vl, counts, q, m, acc, offset, pieces):
+        total = acc[h] * jnp.concatenate([factor, factor], axis=1) + total
+    if keep:
+        acc[h] = total
+        m[h] = peak
+    return total
+
+
+def piece_lives(shape, vl, counts, offset):
     owner = lax.axis_index("ctx") ^ offset
     core = lax.axis_index("sub")
     lives = []
@@ -148,59 +148,44 @@
         for j in range(shape.per_core):
             slot = owner * shape.vertical + source * shape.per_core + j
             lives.append(listed(vl, counts[0, 0], slot))
-    any_live = functools.reduce(jnp.maximum, lives)
-
-    @pl.when(any_live > 0)
-    def _():
-        for h in range(shape.heads):
-            spans = [
-                (piece, pl.ds((j * shape.heads + h) * BLK, BLK))
-                for piece in pieces
-                for j in range(shape.per_core)
-            ]
-            keys = jnp.concatenate([piece[0, span, :] for piece, span in spans], axis=0)
-            values = jnp.concatenate([piece[1, span, :] for piece, span in spans], axis=0)
-            absorb(shape, q, m, acc, h, keys, values, lives)
-
-
-def finish(shape, acc, out, wide):
+    return lives, functools.reduce(jnp.maximum, lives)
+
+
+def piece_head(shape, pieces, which, h):
+    spans = [pl.ds((j * shape.heads + h) * BLK, BLK) for j in range(shape.per_core)]
+    return jnp.concatenate([piece[which, span, :] for piece in pieces for span in spans], axis=0)
+
+
+def store_head(shape, wide, h, total):
     stride = shape.heads * shape.groups
-    for h in range(shape.heads):
-        done = acc[h, :, : shape.dim] / acc[h, :, shape.dim :]
-        for g in range(shape.groups):
-            wide[pl.ds(h * shape.groups + g, shape.tokens, stride=stride), :] = done[
-                g * shape.tokens : (g + 1) * shape.tokens
-            ]
-    out[...] = wide[...].astype(jnp.bfloat16)
+    done = total[:, : shape.dim] / total[:, shape.dim :]
+    for g in range(shape.groups):
+        wide[pl.ds(h * shape.groups + g, shape.tokens, stride=stride), :] = done[
+            g * shape.tokens : (g + 1) * shape.tokens
+        ]
 
 
 def attend_kernel(shape, first, last, offsets, with_fresh, *refs):
     refs = list(refs)
-    vl, sl, counts = refs[:3]
-    refs = refs[3:]
-    if first:
-        raw_q, nk, nv = refs[:3]
-        refs = refs[3:]
+
+    def take(count):
+        taken = refs[:count]
+        del refs[:count]
+        return taken
+
+    vl, sl, counts = take(3)
+    if first:
+        raw_q, nk, nv = take(3)
     else:
-        q, m_in, acc_in = refs[:3]
-        refs = refs[3:]
-    if with_fresh:
-        fresh = refs[: shape.cores]
-        refs = refs[shape.cores :]
-    pieces = []
-    for _ in offsets:
-        pieces.append(refs[: shape.cores])
-        refs = refs[shape.cores :]
-    if first:
-        q, m, acc = refs[:3]
-        refs = refs[3:]
+        q, m, acc = take(3)
+    fresh = take(shape.cores) if with_fresh else []
+    pieces = [take(shape.cores) for _ in offsets]
+    if first:
+        q, m, acc = take(3)
     elif not last:
-        m, acc = refs[:2]
-        refs = refs[2:]
+        m, acc = take(2)
     else:
-        out = refs[0]
-        m, acc = refs[1:3]
-        refs = refs[3:]
+        (out,) = take(1)
     wide_q, wide_kv = refs
 
     if first:
@@ -217,9 +202,6 @@
             keys = split_heads(wide_kv.at[0], BLK, shape.heads, h)
             values = split_heads(wide_kv.at[1], BLK, shape.heads, h)
             absorb(shape, q, m, acc, h, keys, values, [None], causal=True, first=True)
-    else:
-        m[...] = m_in[...]
-        acc[...] = acc_in[...]
 
     if with_fresh:
 
@@ -234,13 +216,29 @@
                 absorb(shape, q, m, acc, h, keys, values, [None])
 
     for offset, arrays in zip(offsets, pieces):
-        absorb_pieces(shape, vl, counts, q, m, acc, offset, arrays)
+        lives, any_live = piece_lives(shape, vl, counts, offset)
+
+        @pl.when(any_live > 0)
+        def _():
+            for h in range(shape.heads):
+                keys = piece_head(shape, arrays, 0, h)
+                values = piece_head(shape, arrays, 1, h)
+                total = absorb(shape, q, m, acc, h, keys, values, lives, keep=not last)
+                if last:
+                    store_head(shape, wide_q, h, total)
+
+        if last:
+
+            @pl.when(any_live == 0)
+            def _():
+                for h in range(shape.heads):
+                    store_head(shape, wide_q, h, acc[h])
 
     if last:
-        finish(shape, acc, out, wide_q)
-
-
-def attend(shape, lists, state, offsets, pieces, fresh=(), first=False, last=False, name=None):
+        out[...] = wide_q[...].astype(jnp.bfloat16)
+
+
+def attend(shape, lists, state, offsets, pieces, fresh=(), first=False, last=False):
     stacked = (shape.heads, shape.rows)
     state_shapes = [
         jax.ShapeDtypeStruct(stacked + (BLK,), jnp.float32),
@@ -256,9 +254,9 @@
         outs = [jax.ShapeDtypeStruct(stacked + (shape.dim,), jnp.bfloat16)] + state_shapes
     elif not last:
         outs = state_shapes
+        aliases = {4: 0, 5: 1}
     else:
         outs = [jax.ShapeDtypeStruct((flat, shape.dim), jnp.bfloat16)]
-        scratch = [VMEM(s.shape, s.dtype) for s in state_shapes] + scratch
     operands = [*lists, *state, *fresh, *[a for arrays in pieces for a in arrays]]
     return pl.pallas_call(
         functools.partial(attend_kernel, shape, first, last, offsets, bool(fresh)),
@@ -268,7 +266,6 @@
         scratch_shapes=scratch,
         input_output_aliases=aliases,
         compiler_params=pltpu.CompilerParams(vmem_limit_bytes=40 << 20),
-        name=name,
     )(*operands)
 
 
@@ -294,24 +291,26 @@
         ]
 
     own, fresh = gather(pool, flat_ck, flat_cv, flat_nk, flat_nv, heads, shape.per_core)
+    order = sorted(range(1, n), key=lambda o: (bin(o).count("1"), -o))
     held = {0: own}
-    order = sorted(range(1, n), key=lambda o: (bin(o).count("1"), -o))
     for offset in order:
         low = offset & -offset
         held[offset] = exchange(held[offset ^ low], low)
     earlier = lax.ppermute(fresh, "ctx", [(i, i + 1) for i in range(n - 1)])
-
+    pieces = {o: both(held[o]) for o in held}
+    fresh = both(earlier)
     state = attend(
-        shape, lists, (flat_q, flat_nk, flat_nv), [0], [both(held[0])], first=True, name="local"
+        shape, lists, (flat_q, flat_nk, flat_nv), [0], [pieces[0]],
+        first=True,
     )
     q = state[0]
     state = attend(
-        shape, lists, state, order[:-1], [both(held[o]) for o in order[:-1]],
-        fresh=both(earlier), name="middle",
+        shape, lists, state, order[:-1], [pieces[o] for o in order[:-1]],
+        fresh=fresh,
     )
     (out,) = attend(
-        shape, lists, (q, *state), order[-1:], [both(held[o]) for o in order[-1:]],
-        last=True, name="tail",
+        shape, lists, (q, *state), order[-1:], [pieces[o] for o in order[-1:]],
+        last=True,
     )
     return out.reshape(queries.shape)
 

time: 40.4 us -> 39.7 us (0.983)
  Pallas kernels: 12.6 us -> 12 us
    pallas_call x3, Pallas kernels: 9.97 us -> 9.33 us  [attend(): pl.pallas_call(functools.partial(attend_kernel, shape, first, last, offse...]
where the time goes in v2:
time: 39.7 us; the launch traced here: 39.5 us
  waiting for transfers between devices  20.1 us (51%)
  Pallas kernels  12 us (30%)
  starting transfers between devices  6.31 us (16%)
  local copies, waits for them, and re-layouts  0.97 us (2%)
    ppermute x3, waiting for transfers between devices, exchange(): return lax.ppermute(x, 'ctx', [(i, i ^ away) for i in range(n)])  19.6 us
    pallas_call x3, Pallas kernels, attend(): pl.pallas_call(functools.partial(attend_kernel, shape, first, last, offse...  9.33 us
    ppermute x5, starting transfers between devices, both(): lax.ppermute(x, 'sub', [(i, i ^ away) for i in range(cores)])  4.71 us
    pallas_call x1, Pallas kernels, gather(): pl.pallas_call(functools.partial(gather_kernel, heads, per_core), out_sha...  2.65 us
    ppermute x1, starting transfers between devices, shards(): earlier = lax.ppermute(fresh, 'ctx', [(i, i + 1) for i in range(n - 1)])  1.28 us
    unnamed x14, local copies, waits for them, and re-layouts  0.97 us
  transfers between devices with their start and end apart: 9, of which 3 were waited for; matrix products, arithmetic and copies ran while one was open for 0% of the time, Pallas kernels for 17%

profile of v2, /device:TPU:31, one launch (start us, length us, event | category | flops | bytes accessed | tf_op | source)
XLA Modules:
  0.0 39.5 jit_solution(13782936821905964917)
XLA Ops:
  0.0 0.0 copy-start
  0.0 0.0 copy-start.1
  0.0 0.0 copy-start.2
  0.0 0.0 copy-start.4
  0.0 0.0 copy-start.5
  0.0 0.0 copy-start.6
  0.0 2.6 %gather.1 = (bf16[2,512,128]{2,1,0:T(8,128)(2,1)}, bf16[512,128]{1,0:T(8,128)(2,1)}) custom-call(s32[2]{0:T(128)} %pool.1, bf16[16,512,128]{2,1,0:T(8,128)(2,1)} %bitcast.11, bf16[16,512,128]{2,1,0:T(8,128)(2,1)} %bitcast.12, bf16[512,128]{1,0:T(8,128)(2,1)} %bitcast.7, bf16[512,128]{1,0:T(8,128)(2,1)} %bitcast.9), custom_call_target="tpu_custom_call" | custom-call | tf_op jit(solution)/shard_map/gather/pallas_call | solution.py:70
  2.7 0.1 collective-permute-start.3
  2.8 0.2 collective-permute-start.5
  3.0 14.6 %collective-permute-done.3.refs_8_ = bf16[2,512,128]{2,1,0:T(8,128)(2,1)S(1)} collective-permute-done((bf16[2,512,128]{2,1,0:T(8,128)(2,1)}, bf16[2,512,128]{2,1,0:T(8,128)(2,1)S(1)}, u32[]{:S(2)}, u32[]{:S(2)}) %collective-permute-start.3) | collective-permute-done | bytes 262176 | tf_op jit(solution)/shard_map/ppermute | solution.py:285
  17.6 0.0 collective-permute-start.7
  17.6 0.5 %collective-permute-start = (bf16[2,512,128]{2,1,0:T(8,128)(2,1)}, bf16[2,512,128]{2,1,0:T(8,128)(2,1)S(1)}, u32[]{:S(2)}, u32[]{:S(2)}) collective-permute-start(bf16[2,512,128]{2,1,0:T(8,128)(2,1)} %get-tuple-element.12.refs_6_), channel_id=1, source_target_pairs={{0,1},{1,0},{2,3},{3,2},{4,5},{5,4},{6,7},{7,6},{8,9},{9,8},{10,11... | collective-permute-start | bytes 786440 | tf_op jit(solution)/shard_map/ppermute | solution.py:289
  18.1 1.3 %collective-permute-start.1 = (bf16[512,128]{1,0:T(8,128)(2,1)}, bf16[512,128]{1,0:T(8,128)(2,1)S(1)}, u32[]{:S(2)}, u32[]{:S(2)}) collective-permute-start(bf16[512,128]{1,0:T(8,128)(2,1)} %get-tuple-element.16), channel_id=1, source_target_pairs={{0,4},{4,8},{8,12},{1,5},{5,9},{9,13},{2,6},{6,10},{10,14},{3,7},{... | collective-permute-start | bytes 393224 | tf_op jit(solution)/shard_map/ppermute | solution.py:299
  19.4 0.1 collective-permute-start.4
  19.5 0.0 collective-permute-done.5.refs_10_
  19.5 0.5 %collective-permute-start.6 = (bf16[2,512,128]{2,1,0:T(8,128)(2,1)S(1)}, bf16[2,512,128]{2,1,0:T(8,128)(2,1)S(1)}, u32[]{:S(2)}, u32[]{:S(2)}) collective-permute-start(bf16[2,512,128]{2,1,0:T(8,128)(2,1)S(1)} %collective-permute-done.5.refs_10_), channel_id=1, source_target_pairs={{0,1},{1,0},{2,3},{3,2},{4,5},{5,4},{6,7},{7,6},{8,9},{9,8},{10,11... | collective-permute-start | bytes 786440 | tf_op jit(solution)/shard_map/ppermute | solution.py:289
  20.0 5.0 %collective-permute-done.7.refs_6_ = bf16[2,512,128]{2,1,0:T(8,128)(2,1)S(1)} collective-permute-done((bf16[2,512,128]{2,1,0:T(8,128)(2,1)S(1)}, bf16[2,512,128]{2,1,0:T(8,128)(2,1)S(1)}, u32[]{:S(2)}, u32[]{:S(2)}) %collective-permute-start.7) | collective-permute-done | bytes 262176 | tf_op jit(solution)/shard_map/ppermute | solution.py:285
  25.0 2.3 %collective-permute-start.8 = (bf16[2,512,128]{2,1,0:T(8,128)(2,1)S(1)}, bf16[2,512,128]{2,1,0:T(8,128)(2,1)S(1)}, u32[]{:S(2)}, u32[]{:S(2)}) collective-permute-start(bf16[2,512,128]{2,1,0:T(8,128)(2,1)S(1)} %collective-permute-done.7.refs_6_), channel_id=1, source_target_pairs={{0,1},{1,0},{2,3},{3,2},{4,5},{5,4},{6,7},{7,6},{8,9},{9,8},{10,11... | collective-permute-start | bytes 786440 | tf_op jit(solution)/shard_map/ppermute | solution.py:289
  27.3 0.5 %collective-permute-done.1.refs_6_ = bf16[512,128]{1,0:T(8,128)(2,1)S(1)} collective-permute-done((bf16[512,128]{1,0:T(8,128)(2,1)}, bf16[512,128]{1,0:T(8,128)(2,1)S(1)}, u32[]{:S(2)}, u32[]{:S(2)}) %collective-permute-start.1) | collective-permute-done | bytes 131104 | tf_op jit(solution)/shard_map/ppermute | solution.py:299
  27.8 1.3 %collective-permute-start.2 = (bf16[512,128]{1,0:T(8,128)(2,1)S(1)}, bf16[512,128]{1,0:T(8,128)(2,1)S(1)}, u32[]{:S(2)}, u32[]{:S(2)}) collective-permute-start(bf16[512,128]{1,0:T(8,128)(2,1)S(1)} %collective-permute-done.1.refs_6_), channel_id=1, source_target_pairs={{0,1},{1,0},{2,3},{3,2},{4,5},{5,4},{6,7},{7,6},{8,9},{9,8},{10,11... | collective-permute-start | bytes 393224 | tf_op jit(solution)/shard_map/ppermute | solution.py:289
  29.1 0.0 collective-permute-done.refs_7_
  29.1 0.0 copy-done
  29.1 0.0 copy-done.1
  29.1 0.0 copy-done.2
  29.2 0.0 copy-done.4
  29.2 0.0 copy-done.5
  29.2 0.0 copy-done.6
  29.2 0.0 copy-start.3
  29.2 0.9 %copy-done.3 = bf16[2,512,128]{2,1,0:T(8,128)(2,1)S(1)} copy-done((bf16[2,512,128]{2,1,0:T(8,128)(2,1)S(1)}, bf16[2,512,128]{2,1,0:T(8,128)(2,1)}, u32[]{:S(2)}) %copy-start.3) | copy-done | bytes 262168
  30.1 2.9 %shard_map.91 = (bf16[4,512,128]{2,1,0:T(8,128)(2,1)S(1)}, f32[4,512,128]{2,1,0:T(8,128)S(1)}, f32[4,512,256]{2,1,0:T(8,128)S(1)}) custom-call(s32[1,6]{1,0:T(1,128)S(1)} %copy-done.4, s32[1,2]{1,0:T(1,128)S(1)} %copy-done.5, s32[1,2]{1,0:T(1,128)S(1)} %copy-done.6, bf16[2048,128]{1,0:T(8,128)(2,1)S(1)} %bitcast.6, bf16[512,128]{1,0:T(8,128)(2,1)S(1)} %bitcast.8, ...), custom_call_target="tpu_custom_call" | custom-call | tf_op jit(solution)/shard_map/pallas_call | solution.py:261
  33.0 0.0 collective-permute-done.2.refs_7_
  33.0 0.0 collective-permute-done.4.refs_9_
  33.0 0.0 collective-permute-done.6.refs_11_
  33.0 3.8 %shard_map.92 = (f32[4,512,128]{2,1,0:T(8,128)S(1)}, f32[4,512,256]{2,1,0:T(8,128)S(1)}) custom-call(s32[1,6]{1,0:T(1,128)S(1)} %copy-done.4, s32[1,2]{1,0:T(1,128)S(1)} %copy-done.5, s32[1,2]{1,0:T(1,128)S(1)} %copy-done.6, bf16[4,512,128]{2,1,0:T(8,128)(2,1)S(1)} %get-tuple-element.13.refs_3_, ...), custom_call_target="tpu_custom_call", output_to_operand_aliasing={{0}: (4, {}), {1}: (5, {})} | custom-call | tf_op jit(solution)/shard_map/pallas_call | solution.py:261
  36.8 0.0 collective-permute-done.8.refs_7_
  36.8 2.7 %shard_map.93 = bf16[2048,128]{1,0:T(8,128)(2,1)} custom-call(s32[1,6]{1,0:T(1,128)S(1)} %copy-done.4, s32[1,2]{1,0:T(1,128)S(1)} %copy-done.5, s32[1,2]{1,0:T(1,128)S(1)} %copy-done.6, bf16[4,512,128]{2,1,0:T(8,128)(2,1)S(1)} %get-tuple-element.13.refs_3_, f32[4,512,128]{2,1,0:T(8,128)S(1)} %get-tuple-element.17.refs_4_, ...), custom_call_target="tpu_custom_call" | custom-call | tf_op jit(solution)/shard_map/pallas_call | solution.py:261
Async XLA Ops:
  0.0 29.1 %copy-start = (bf16[128,4,4,128]{3,2,1,0:T(4,128)(2,1)S(1)}, bf16[128,4,4,128]{3,2,1,0:T(4,128)(2,1)}, u32[]{:S(2)}) copy-start(bf16[128,4,4,128]{3,2,1,0:T(4,128)(2,1)} %param.9) | copy-start | bytes 1572868
  0.0 29.1 %copy-start.1 = (bf16[128,4,128]{2,1,0:T(4,128)(2,1)S(1)}, bf16[128,4,128]{2,1,0:T(4,128)(2,1)}, u32[]{:S(2)}) copy-start(bf16[128,4,128]{2,1,0:T(4,128)(2,1)} %param.10) | copy-start | bytes 393220
  0.0 29.1 %copy-start.2 = (bf16[128,4,128]{2,1,0:T(4,128)(2,1)S(1)}, bf16[128,4,128]{2,1,0:T(4,128)(2,1)}, u32[]{:S(2)}) copy-start(bf16[128,4,128]{2,1,0:T(4,128)(2,1)} %param.11) | copy-start | bytes 393220
  0.0 29.1 %copy-start.4 = (s32[1,6]{1,0:T(1,128)S(1)}, s32[1,6]{1,0:T(1,128)}, u32[]{:S(2)}) copy-start(s32[1,6]{1,0:T(1,128)} %refs_0_.5) | copy-start | bytes 76
  0.0 29.1 %copy-start.5 = (s32[1,2]{1,0:T(1,128)S(1)}, s32[1,2]{1,0:T(1,128)}, u32[]{:S(2)}) copy-start(s32[1,2]{1,0:T(1,128)} %refs_1_.5) | copy-start | bytes 28
  0.0 29.1 %copy-start.6 = (s32[1,2]{1,0:T(1,128)S(1)}, s32[1,2]{1,0:T(1,128)}, u32[]{:S(2)}) copy-start(s32[1,2]{1,0:T(1,128)} %refs_2_.5) | copy-start | bytes 28
  2.7 14.9 %collective-permute-start.3 = (bf16[2,512,128]{2,1,0:T(8,128)(2,1)}, bf16[2,512,128]{2,1,0:T(8,128)(2,1)S(1)}, u32[]{:S(2)}, u32[]{:S(2)}) collective-permute-start(bf16[2,512,128]{2,1,0:T(8,128)(2,1)} %get-tuple-element.12.refs_6_), channel_id=1, source_target_pairs={{0,8},{4,12},{8,0},{12,4},{1,9},{5,13},{9,1},{13,5},{2,10},{6,14},... | collective-permute-start | bytes 786440 | tf_op jit(solution)/shard_map/ppermute | solution.py:285
  2.8 16.7 %collective-permute-start.5 = (bf16[2,512,128]{2,1,0:T(8,128)(2,1)}, bf16[2,512,128]{2,1,0:T(8,128)(2,1)S(1)}, u32[]{:S(2)}, u32[]{:S(2)}) collective-permute-start(bf16[2,512,128]{2,1,0:T(8,128)(2,1)} %get-tuple-element.12.refs_6_), channel_id=1, source_target_pairs={{0,4},{4,0},{8,12},{12,8},{1,5},{5,1},{9,13},{13,9},{2,6},{6,2},{1... | collective-permute-start | bytes 786440 | tf_op jit(solution)/shard_map/ppermute | solution.py:285
  17.6 7.4 %collective-permute-start.7 = (bf16[2,512,128]{2,1,0:T(8,128)(2,1)S(1)}, bf16[2,512,128]{2,1,0:T(8,128)(2,1)S(1)}, u32[]{:S(2)}, u32[]{:S(2)}) collective-permute-start(bf16[2,512,128]{2,1,0:T(8,128)(2,1)S(1)} %collective-permute-done.3.refs_8_), channel_id=1, source_target_pairs={{0,4},{4,0},{8,12},{12,8},{1,5},{5,1},{9,13},{13,9},{2,6},{6,2},{1... | collective-permute-start | bytes 786440 | tf_op jit(solution)/shard_map/ppermute | solution.py:285
  17.6 11.5 %collective-permute-start = (bf16[2,512,128]{2,1,0:T(8,128)(2,1)}, bf16[2,512,128]{2,1,0:T(8,128)(2,1)S(1)}, u32[]{:S(2)}, u32[]{:S(2)}) collective-permute-start(bf16[2,512,128]{2,1,0:T(8,128)(2,1)} %get-tuple-element.12.refs_6_), channel_id=1, source_target_pairs={{0,1},{1,0},{2,3},{3,2},{4,5},{5,4},{6,7},{7,6},{8,9},{9,8},{10,11... | collective-permute-start | bytes 786440 | tf_op jit(solution)/shard_map/ppermute | solution.py:289
  18.1 9.7 %collective-permute-start.1 = (bf16[512,128]{1,0:T(8,128)(2,1)}, bf16[512,128]{1,0:T(8,128)(2,1)S(1)}, u32[]{:S(2)}, u32[]{:S(2)}) collective-permute-start(bf16[512,128]{1,0:T(8,128)(2,1)} %get-tuple-element.16), channel_id=1, source_target_pairs={{0,4},{4,8},{8,12},{1,5},{5,9},{9,13},{2,6},{6,10},{10,14},{3,7},{... | collective-permute-start | bytes 393224 | tf_op jit(solution)/shard_map/ppermute | solution.py:299
  19.4 13.6 %collective-permute-start.4 = (bf16[2,512,128]{2,1,0:T(8,128)(2,1)S(1)}, bf16[2,512,128]{2,1,0:T(8,128)(2,1)S(1)}, u32[]{:S(2)}, u32[]{:S(2)}) collective-permute-start(bf16[2,512,128]{2,1,0:T(8,128)(2,1)S(1)} %collective-permute-done.3.refs_8_), channel_id=1, source_target_pairs={{0,1},{1,0},{2,3},{3,2},{4,5},{5,4},{6,7},{7,6},{8,9},{9,8},{10,11... | collective-permute-start | bytes 786440 | tf_op jit(solution)/shard_map/ppermute | solution.py:289
  19.5 13.6 %collective-permute-start.6 = (bf16[2,512,128]{2,1,0:T(8,128)(2,1)S(1)}, bf16[2,512,128]{2,1,0:T(8,128)(2,1)S(1)}, u32[]{:S(2)}, u32[]{:S(2)}) collective-permute-start(bf16[2,512,128]{2,1,0:T(8,128)(2,1)S(1)} %collective-permute-done.5.refs_10_), channel_id=1, source_target_pairs={{0,1},{1,0},{2,3},{3,2},{4,5},{5,4},{6,7},{7,6},{8,9},{9,8},{10,11... | collective-permute-start | bytes 786440 | tf_op jit(solution)/shard_map/ppermute | solution.py:289
  25.0 11.9 %collective-permute-start.8 = (bf16[2,512,128]{2,1,0:T(8,128)(2,1)S(1)}, bf16[2,512,128]{2,1,0:T(8,128)(2,1)S(1)}, u32[]{:S(2)}, u32[]{:S(2)}) collective-permute-start(bf16[2,512,128]{2,1,0:T(8,128)(2,1)S(1)} %collective-permute-done.7.refs_6_), channel_id=1, source_target_pairs={{0,1},{1,0},{2,3},{3,2},{4,5},{5,4},{6,7},{7,6},{8,9},{9,8},{10,11... | collective-permute-start | bytes 786440 | tf_op jit(solution)/shard_map/ppermute | solution.py:289
  27.8 5.2 %collective-permute-start.2 = (bf16[512,128]{1,0:T(8,128)(2,1)S(1)}, bf16[512,128]{1,0:T(8,128)(2,1)S(1)}, u32[]{:S(2)}, u32[]{:S(2)}) collective-permute-start(bf16[512,128]{1,0:T(8,128)(2,1)S(1)} %collective-permute-done.1.refs_6_), channel_id=1, source_target_pairs={{0,1},{1,0},{2,3},{3,2},{4,5},{5,4},{6,7},{7,6},{8,9},{9,8},{10,11... | collective-permute-start | bytes 393224 | tf_op jit(solution)/shard_map/ppermute | solution.py:289
  29.2 1.0 %copy-start.3 = (bf16[2,512,128]{2,1,0:T(8,128)(2,1)S(1)}, bf16[2,512,128]{2,1,0:T(8,128)(2,1)}, u32[]{:S(2)}) copy-start(bf16[2,512,128]{2,1,0:T(8,128)(2,1)} %get-tuple-element.12.refs_6_) | copy-start | bytes 786436
